TPU v7x, 256 devices: a whole 4x4x8 slice. The times are simulated.
256 devices in a mesh: seq: 16 (over z, x_hi), mp: 16 (over y, x_lo, core).
Axes of the slice: x: 4 (x_hi: 2, x_lo: 2; x = x_hi * 2 + x_lo), y: 4, z: 8, core: 2. Of those that a mesh axis runs over, the one named last changes fastest.
Arguments:
- tokens: bfloat16 [8192, 4608], P('seq', 'mp')
- pre_gain: bfloat16 [4608], P('mp'), may hold values from -2.5 to 2.5
- post_gain: bfloat16 [4608], P('mp'), may hold values from -2.5 to 2.5
- w_query: bfloat16 [4608, 4096], P('seq', 'mp')
- w_key: bfloat16 [4608, 2048], P('seq', 'mp')
- w_value: bfloat16 [4608, 2048], P('seq', 'mp'), may hold values from -0.09375 to 0.09375
- w_out: bfloat16 [4096, 4608], P('mp', 'seq')
- segment_ids: int32 [8192], P('seq'), may hold values from 0 to 3, never falling along the last dimension, each value on 1 to 6553 neighbouring positions
- page_table: int32 [64], P('seq'), may hold values from 0 to 63, as said below
Outputs:
- layer_output: bfloat16 [8192, 4608], P('seq', 'mp')
- key_cache: bfloat16 [64, 128, 2048], P('seq', None, 'mp')
- value_cache: bfloat16 [64, 128, 2048], P('seq', None, 'mp')
Inputs may be any that keep to these rules, and one draw needn't show every extreme that they name: segment_ids never fall along the stream, every tenant of 0 to 3 is present, each has at least 1 and at most 6553 tokens and one has exactly 6553. page_table is a permutation; the slot of page p lies in the same block of 4 slots as p, that is page_table[p] // 4 = p // 4.
All inputs are finite; a program needn't handle non-finite values.
Results may differ from a plain program's by a relative error of at most 0.019.
Values may be sent and summed in bfloat16 or wider, within the bound.
No kernel may reach another device: no remote copies, remote signals or barrier semaphores. Data moves between devices by JAX's collectives and lax.ppermute only.
A program may use at most 64 MiB of HBM per device.

v0:
```python
import math
import jax
import jax.numpy as jnp
from jax import lax
from jax.sharding import PartitionSpec as P

D = 4608
HQ = 32
HD = 128
WINDOW = 4096
PAGE = 128
SEGS = 4
EPSILON = 1e-06
SOFT_CAP = 50.0
LARGE_INDEX = 1 << 30


def from_behind(block, axis, distance):
    devices = range(lax.axis_size(axis))
    route = [(i - distance, i) for i in devices if i - distance in devices]
    return lax.ppermute(block, axis, route)


def rotate(values, positions):
    half = values.shape[-1] // 2
    freqs = jnp.exp(
        -math.log(10000.0) * jnp.arange(half, dtype=jnp.float32) * (2.0 / values.shape[-1])
    )
    angles = positions.astype(jnp.float32)[:, None] * freqs[None, :]
    cosine = jnp.cos(angles)[:, None, :]
    sine = jnp.sin(angles)[:, None, :]
    first = values[..., :half]
    second = values[..., half:]
    return jnp.concatenate(
        [first * cosine - second * sine, second * cosine + first * sine], axis=-1
    )


def add_product(normed, piece):
    return jnp.dot(normed, piece, preferred_element_type=jnp.float32)


def shards(tokens, pre_gain, post_gain, w_query, w_key, w_value, w_out, segment_ids, page_table):
    rows_here = tokens.shape[0]
    whole, gain_full = (
        lax.all_gather(tokens, "mp", axis=1, tiled=True),
        lax.all_gather(pre_gain, "mp", axis=0, tiled=True),
    )
    x_whole = whole.astype(jnp.float32)
    pre_scale = lax.rsqrt(jnp.mean(x_whole * x_whole, axis=1, keepdims=True) + EPSILON)
    normed = (x_whole * pre_scale * (1.0 + gain_full.astype(jnp.float32))[None, :]).astype(
        jnp.bfloat16
    )
    query_raw = add_product(normed, lax.all_gather(w_query, "seq", axis=0, tiled=True))
    key_raw = add_product(normed, lax.all_gather(w_key, "seq", axis=0, tiled=True))
    value_raw = add_product(normed, lax.all_gather(w_value, "seq", axis=0, tiled=True))
    heads_query = w_query.shape[1] // HD
    heads_kv = w_key.shape[1] // HD
    seq_index = lax.axis_index("seq")
    base = seq_index * rows_here
    global_index = base + jnp.arange(rows_here, dtype=jnp.int32)
    local_first = jnp.stack(
        [jnp.min(jnp.where(segment_ids == s, global_index, LARGE_INDEX)) for s in range(SEGS)]
    )
    starts = lax.pmin(local_first, "seq")
    offsets = jnp.zeros((rows_here,), jnp.int32)
    for s in range(SEGS):
        offsets = offsets + jnp.where(segment_ids == s, starts[s], 0)
    within = global_index - offsets
    query_scale = float(D // HQ) ** (-0.5)
    queries = (rotate(query_raw.reshape(rows_here, heads_query, HD), within) * query_scale).astype(
        jnp.bfloat16
    )
    keys_here = rotate(key_raw.reshape(rows_here, heads_kv, HD), within).astype(jnp.bfloat16)
    values_here = value_raw.reshape(rows_here, heads_kv, HD).astype(jnp.bfloat16)
    reach = WINDOW // rows_here
    earlier = []
    current = (keys_here, values_here)
    for distance in range(reach):
        current = from_behind((current[0], current[1]), "seq", 1)
        earlier.append(current)
    earlier = earlier[::-1]
    keys_all = jnp.concatenate([pair[0] for pair in earlier] + [keys_here], axis=0)
    values_all = jnp.concatenate([pair[1] for pair in earlier] + [values_here], axis=0)
    block = math.gcd(rows_here, 512)
    grouped = queries.reshape(rows_here, heads_kv, heads_query // heads_kv, HD)

    def attend(start):
        query_pos = base + start + jnp.arange(block, dtype=jnp.int32)
        key_pos = base - WINDOW + start + jnp.arange(WINDOW + block, dtype=jnp.int32)
        key_segment = jnp.zeros((WINDOW + block,), jnp.int32)
        for s in range(1, SEGS):
            key_segment = key_segment + (key_pos >= starts[s]).astype(jnp.int32)
        distance = query_pos[:, None] - key_pos[None, :]
        allowed = (
            (key_pos >= 0)[None, :]
            & (distance >= 0)
            & (distance < WINDOW)
            & (segment_ids[:, None] == key_segment[None, :])
        )
        scores = jnp.einsum("qgrd,kgd->grqk", grouped, keys_all, preferred_element_type=jnp.float32)
        capped = SOFT_CAP * jnp.tanh(scores / SOFT_CAP)
        weights = jnp.where(allowed[None, None], jnp.exp(capped), 0.0)
        denominator = jnp.sum(weights, axis=-1)
        rounded = weights.astype(jnp.bfloat16)
        summed = jnp.einsum(
            "grqk,kgd->qgrd", rounded, values_all, preferred_element_type=jnp.float32
        )
        result = summed / jnp.transpose(denominator, (2, 0, 1))[..., None]
        return result.astype(jnp.bfloat16).reshape(block, heads_query * HD)

    block_starts = jnp.arange(rows_here // block, dtype=jnp.int32) * block
    attended = lax.map(attend, block_starts).reshape(rows_here, heads_query * HD)
    group_terms = jnp.dot(
        attended,
        lax.all_gather(w_out, "seq", axis=1, tiled=True),
        preferred_element_type=jnp.float32,
    )
    attention_share = lax.psum_scatter(
        group_terms.astype(jnp.bfloat16), "mp", scatter_dimension=1, tiled=True
    ).astype(jnp.float32)
    squares = jnp.sum(attention_share * attention_share, axis=1)
    square_total = lax.psum(squares, "mp")
    post_scale = lax.rsqrt(square_total / D + EPSILON)
    post = attention_share * post_scale[:, None] * (1.0 + post_gain.astype(jnp.float32))[None, :]
    layer_output = (tokens.astype(jnp.float32) + post).astype(jnp.bfloat16)
    pages_here = page_table.shape[0]
    local_slot = page_table - seq_index * pages_here
    one_hot = (local_slot[None, :] == jnp.arange(pages_here, dtype=jnp.int32)[:, None]).astype(
        jnp.bfloat16
    )
    stacked = jnp.stack(
        [
            keys_here.reshape(pages_here, PAGE, heads_kv * HD),
            values_here.reshape(pages_here, PAGE, heads_kv * HD),
        ]
    )
    placed = jnp.einsum(
        "sp,tpce->tsce", one_hot, stacked, preferred_element_type=jnp.float32
    ).astype(jnp.bfloat16)
    return (layer_output, placed[0], placed[1])


def solution(mesh):
    return jax.shard_map(
        shards,
        mesh=mesh,
        in_specs=(
            P("seq", "mp"),
            P("mp"),
            P("mp"),
            P("seq", "mp"),
            P("seq", "mp"),
            P("seq", "mp"),
            P("mp", "seq"),
            P("seq"),
            P("seq"),
        ),
        out_specs=(P("seq", "mp"), P("seq", None, "mp"), P("seq", None, "mp")),
        check_vma=False,
    )
```

profile of v0, /device:TPU:32, one launch (start us, length us, event | category | flops | bytes accessed | tf_op | source)
XLA Modules:
  0.0 506.7 jit_solution(7526832199181364429)
XLA Ops:
  14.0 19.3 %pmin.7 = s32[4]{0:T(128)S(1)} all-reduce(s32[4]{0:T(128)S(1)} %pad_add_fusion), channel_id=1, replica_groups=mesh['seq'=16,'mp'=16] {'seq'}, use_global_device_ids=true, to_apply=%region_5.6 | all-reduce | flops 4 | bytes 32 | tf_op jit(solution)/shard_map/pmin | solution.py:65
  36.1 53.1 %all-reduce = bf16[4608]{0:T(1024)(128)(2,1)S(1)} all-reduce(bf16[4608]{0:T(1024)(128)(2,1)S(1)} %dynamic-update-slice), channel_id=1, replica_groups=mesh['seq'=16,'mp'=16] {'mp'}, use_global_device_ids=true, to_apply=%add | all-reduce | flops 4608 | bytes 18432
  95.9 39.3 %all-gather.10.cloned.1.call-done = bf16[4608,128]{1,0:T(8,128)(2,1)} async-done(((bf16[288,128]{1,0:T(8,128)(2,1)}), bf16[4608,128]{1,0:T(8,128)(2,1)}) %all-gather.10.cloned.1.call-update) | async-done | bytes 1179664 | tf_op jit(solution)/shard_map/all_gather | solution.py:55
  135.2 4.4 convolution_bitcast_fusion
  142.7 71.6 %all-gather.8.cloned.1.call-done = bf16[4608,128]{1,0:T(8,128)(2,1)} async-done(((bf16[288,128]{1,0:T(8,128)(2,1)}), bf16[4608,128]{1,0:T(8,128)(2,1)}) %all-gather.8.cloned.1.call-update) | async-done | bytes 1179664 | tf_op jit(solution)/shard_map/all_gather | solution.py:56
  214.3 4.8 convolution_convert_fusion.2
  221.7 5.4 %collective-permute-start.9 = (bf16[512,1,128]{0,2,1:T(8,128)(2,1)S(1)}, bf16[512,1,128]{0,2,1:T(8,128)(2,1)S(1)}, u32[]{:S(2)}, u32[]{:S(2)}) collective-permute-start(bf16[512,1,128]{0,2,1:T(8,128)(2,1)S(1)} %collective-permute-done.8), channel_id=1, source_target_pairs={{0,16},{16,32},{32,48},{48,64},{64,80},{80,96},{96,112},{112,128},... | collective-permute-start | bytes 393224 | tf_op jit(solution)/shard_map/ppermute | solution.py:21
  232.1 4.3 collective-permute-start.10
  247.3 5.2 %fusion.10 = pred[512,4608]{0,1:T(8,128)(4,1)S(1)} fusion(s32[512]{0:T(512)S(1)} %copy-done.21, s32[4608]{0:T(1024)S(1)} %get-tuple-element.61, s32[512]{0:T(512)S(1)} %iota_add_fusion.1, s32[4608]{0:T(1024)S(1)} %get-tuple-element.60, pred[4608]{0:T(1024)(128)(4,1)S(1)} %fusion.52), kind=kLoop, calls=%fused_computation.14 | loop fusion | flops 16515072 | bytes 2404864 | tf_op jit(solution)/shard_map/while/body/eval_jaxpr/and | solution.py:96
  252.5 4.0 collective-permute-start.3
  256.5 4.7 collective-permute-start.12
  263.0 4.3 collective-permute-start.4
  267.3 4.3 collective-permute-start.13
  271.7 32.8 %all-gather.12.cloned.1.call-done = bf16[4608,256]{1,0:T(8,128)(2,1)} async-done(((bf16[288,256]{1,0:T(8,128)(2,1)}), bf16[4608,256]{1,0:T(8,128)(2,1)}) %all-gather.12.cloned.1.call-update) | async-done | bytes 2359312 | tf_op jit(solution)/shard_map/all_gather | solution.py:54
  304.5 4.9 fusion.62
  311.8 5.1 %collective-permute-start.14 = (bf16[512,1,128]{0,2,1:T(8,128)(2,1)}, bf16[512,1,128]{0,2,1:T(8,128)(2,1)}, u32[]{:S(2)}, u32[]{:S(2)}) collective-permute-start(bf16[512,1,128]{0,2,1:T(8,128)(2,1)} %collective-permute-done.13), channel_id=1, source_target_pairs={{0,16},{16,32},{32,48},{48,64},{64,80},{80,96},{96,112},{112,128},... | collective-permute-start | bytes 393224 | tf_op jit(solution)/shard_map/ppermute | solution.py:21
  322.2 6.0 %collective-permute-start.15 = (bf16[512,1,128]{0,2,1:T(8,128)(2,1)}, bf16[512,1,128]{0,2,1:T(8,128)(2,1)S(1)}, u32[]{:S(2)}, u32[]{:S(2)}) collective-permute-start(bf16[512,1,128]{0,2,1:T(8,128)(2,1)} %collective-permute-done.14), channel_id=1, source_target_pairs={{0,16},{16,32},{32,48},{48,64},{64,80},{80,96},{96,112},{112,128},... | collective-permute-start | bytes 393224 | tf_op jit(solution)/shard_map/ppermute | solution.py:21
  335.1 4.2 collective-permute-done.7
  341.4 6.7 %fusion = (f32[2,512]{1,0:T(2,128)S(1)}, f32[4608,512,2]{1,0,2:T(8,128)S(1)}) fusion(pred[512,4608]{0,1:T(8,128)(4,1)S(1)} %fusion.10, f32[512,2,64]{2,0,1:T(8,128)S(1)} %get-tuple-element.39, f32[512,2,64]{2,0,1:T(8,128)S(1)} %get-tuple-element.38, bf16[4608,1,128]{0,2,1:T(8,128)(2,1)S(1)} %constant_dynamic-update-slice_fusion.9), kind=kOutput, calls=%fused_computation.3 | convolution fusion | flops 1227226112 | bytes 22941696 | tf_op jit(solution)/shard_map/while/body/eval_jaxpr/qgrd,kgd->grqk/dot_general | solution.py:101
  348.1 6.3 %fusion.24 = bf16[512,1,2,128]{0,3,2,1:T(8,128)(2,1)S(1)} fusion(f32[4608,512,2]{1,0,2:T(8,128)S(1)} %get-tuple-element.59, pred[512,4608]{0,1:T(8,128)(4,1)S(1)} %fusion.10, bf16[4608,1,128]{2,0,1:T(8,128)(2,1)S(1)} %constant_dynamic-update-slice_fusion, f32[512,2]{0,1:T(2,128)S(1)} %bitcast.95), kind=kOutput, calls=%fused_computation.26 | convolution fusion | flops 1227096064 | bytes 22679552 | tf_op jit(solution)/shard_map/while/body/eval_jaxpr/grqk,kgd->qgrd/dot_general | solution.py:106
  354.5 37.5 %all-gather.14.cloned.1.call-done = bf16[256,4608]{0,1:T(8,128)(2,1)} async-done(((bf16[256,288]{0,1:T(8,128)(2,1)}), bf16[256,4608]{0,1:T(8,128)(2,1)}) %all-gather.14.cloned.1.call-update) | async-done | bytes 2359312 | tf_op jit(solution)/shard_map/all_gather | solution.py:116
  391.9 5.2 %convolution_convert_fusion = bf16[512,4608]{0,1:T(8,128)(2,1)} fusion(bf16[256,4608]{0,1:T(8,128)(2,1)} %all-gather.14.cloned.1.call-done, bf16[512,256]{0,1:T(8,128)(2,1)S(1)} %bitcast.94), kind=kOutput, calls=%fused_computation.16 | convolution fusion | flops 1210318848 | bytes 7340032 | tf_op jit(solution)/shard_map/dot_general | solution.py:114
  400.1 67.7 %reduce-scatter.2.cloned.1.call-done = bf16[512,288]{0,1:T(8,128)(2,1)} async-done(((bf16[512,4608]{0,1:T(8,128)(2,1)}), bf16[512,288]{0,1:T(8,128)(2,1)}) %reduce-scatter.2.cloned.1.call-update) | async-done | bytes 294928 | tf_op jit(solution)/shard_map/reduce_scatter | solution.py:119
  468.9 29.2 %psum.7 = f32[512]{0:T(512)S(1)} all-reduce(f32[512]{0:T(512)S(1)} %fusion.29), channel_id=1, replica_groups=mesh['seq'=16,'mp'=16] {'mp'}, use_global_device_ids=true, to_apply=%region_9.10 | all-reduce | flops 512 | bytes 4096 | tf_op jit(solution)/shard_map/psum | solution.py:123
  (137 shorter events, 60.9 us)
Async XLA Ops:
  7.2 85.3 %all-gather.6.cloned.1.call-start = ((), (), s32[]{:S(2)}) async-start(), calls=%async_computation.1 | async-start | bytes 5013504 | tf_op jit(solution)/shard_map/all_gather | solution.py:46
  7.9 127.3 %all-gather.10.cloned.1.call-start = ((), (), s32[]{:S(2)}) async-start(), calls=%async_computation.3 | async-start | bytes 1253376 | tf_op jit(solution)/shard_map/all_gather | solution.py:55
  8.6 205.7 %all-gather.8.cloned.1.call-start = ((), (), s32[]{:S(2)}) async-start(), calls=%async_computation.2 | async-start | bytes 1253376 | tf_op jit(solution)/shard_map/all_gather | solution.py:56
  9.4 295.1 %all-gather.12.cloned.1.call-start = ((), (), s32[]{:S(2)}) async-start(), calls=%async_computation.4 | async-start | bytes 2506752 | tf_op jit(solution)/shard_map/all_gather | solution.py:54
  10.0 382.0 %all-gather.14.cloned.1.call-start = ((), (), s32[]{:S(2)}) async-start(), calls=%async_computation.5 | async-start | bytes 2506752 | tf_op jit(solution)/shard_map/all_gather | solution.py:116
  140.2 107.1 %copy-start.21 = (s32[512]{0:T(512)S(1)}, s32[512]{0:T(512)}, u32[]{:S(2)}) copy-start(s32[512]{0:T(512)} %param.16) | copy-start | bytes 6148
  140.2 81.4 %collective-permute-start.8 = (bf16[512,1,128]{0,2,1:T(8,128)(2,1)S(1)}, bf16[512,1,128]{0,2,1:T(8,128)(2,1)S(1)}, u32[]{:S(2)}, u32[]{:S(2)}) collective-permute-start(bf16[512,1,128]{0,2,1:T(8,128)(2,1)S(1)} %pad_maximum_fusion), channel_id=1, source_target_pairs={{0,16},{16,32},{32,48},{48,64},{64,80},{80,96},{96,112},{112,128},... | collective-permute-start | bytes 393224 | tf_op jit(solution)/shard_map/ppermute | solution.py:21
  219.2 9.3 %collective-permute-start = (bf16[512,1,128]{2,0,1:T(8,128)(2,1)S(1)}, bf16[512,1,128]{2,0,1:T(8,128)(2,1)S(1)}, u32[]{:S(2)}, u32[]{:S(2)}) collective-permute-start(bf16[512,1,128]{2,0,1:T(8,128)(2,1)S(1)} %bitcast.92), channel_id=1, source_target_pairs={{0,16},{16,32},{32,48},{48,64},{64,80},{80,96},{96,112},{112,128},... | collective-permute-start | bytes 393224 | tf_op jit(solution)/shard_map/ppermute | solution.py:21
  221.7 10.4 %collective-permute-start.9 = (bf16[512,1,128]{0,2,1:T(8,128)(2,1)S(1)}, bf16[512,1,128]{0,2,1:T(8,128)(2,1)S(1)}, u32[]{:S(2)}, u32[]{:S(2)}) collective-permute-start(bf16[512,1,128]{0,2,1:T(8,128)(2,1)S(1)} %collective-permute-done.8), channel_id=1, source_target_pairs={{0,16},{16,32},{32,48},{48,64},{64,80},{80,96},{96,112},{112,128},... | collective-permute-start | bytes 393224 | tf_op jit(solution)/shard_map/ppermute | solution.py:21
  227.1 240.7 %reduce-scatter.2.cloned.1.call-start = ((), (), s32[]{:S(2)}) async-start(), calls=%async_computation.6 | async-start | bytes 5013504 | tf_op jit(solution)/shard_map/reduce_scatter | solution.py:119
  228.4 9.9 %collective-permute-start.1 = (bf16[512,1,128]{2,0,1:T(8,128)(2,1)S(1)}, bf16[512,1,128]{2,0,1:T(8,128)(2,1)S(1)}, u32[]{:S(2)}, u32[]{:S(2)}) collective-permute-start(bf16[512,1,128]{2,0,1:T(8,128)(2,1)S(1)} %collective-permute-done), channel_id=1, source_target_pairs={{0,16},{16,32},{32,48},{48,64},{64,80},{80,96},{96,112},{112,128},... | collective-permute-start | bytes 393224 | tf_op jit(solution)/shard_map/ppermute | solution.py:21
  232.1 11.4 %collective-permute-start.10 = (bf16[512,1,128]{0,2,1:T(8,128)(2,1)S(1)}, bf16[512,1,128]{0,2,1:T(8,128)(2,1)S(1)}, u32[]{:S(2)}, u32[]{:S(2)}) collective-permute-start(bf16[512,1,128]{0,2,1:T(8,128)(2,1)S(1)} %collective-permute-done.9), channel_id=1, source_target_pairs={{0,16},{16,32},{32,48},{48,64},{64,80},{80,96},{96,112},{112,128},... | collective-permute-start | bytes 393224 | tf_op jit(solution)/shard_map/ppermute | solution.py:21
  238.4 14.1 %collective-permute-start.2 = (bf16[512,1,128]{2,0,1:T(8,128)(2,1)S(1)}, bf16[512,1,128]{2,0,1:T(8,128)(2,1)S(1)}, u32[]{:S(2)}, u32[]{:S(2)}) collective-permute-start(bf16[512,1,128]{2,0,1:T(8,128)(2,1)S(1)} %collective-permute-done.1), channel_id=1, source_target_pairs={{0,16},{16,32},{32,48},{48,64},{64,80},{80,96},{96,112},{112,128},... | collective-permute-start | bytes 393224 | tf_op jit(solution)/shard_map/ppermute | solution.py:21
  243.5 13.0 %collective-permute-start.11 = (bf16[512,1,128]{0,2,1:T(8,128)(2,1)S(1)}, bf16[512,1,128]{0,2,1:T(8,128)(2,1)S(1)}, u32[]{:S(2)}, u32[]{:S(2)}) collective-permute-start(bf16[512,1,128]{0,2,1:T(8,128)(2,1)S(1)} %collective-permute-done.10), channel_id=1, source_target_pairs={{0,16},{16,32},{32,48},{48,64},{64,80},{80,96},{96,112},{112,128},... | collective-permute-start | bytes 393224 | tf_op jit(solution)/shard_map/ppermute | solution.py:21
  252.5 10.5 %collective-permute-start.3 = (bf16[512,1,128]{2,0,1:T(8,128)(2,1)S(1)}, bf16[512,1,128]{2,0,1:T(8,128)(2,1)S(1)}, u32[]{:S(2)}, u32[]{:S(2)}) collective-permute-start(bf16[512,1,128]{2,0,1:T(8,128)(2,1)S(1)} %collective-permute-done.2), channel_id=1, source_target_pairs={{0,16},{16,32},{32,48},{48,64},{64,80},{80,96},{96,112},{112,128},... | collective-permute-start | bytes 393224 | tf_op jit(solution)/shard_map/ppermute | solution.py:21
  256.5 10.8 %collective-permute-start.12 = (bf16[512,1,128]{0,2,1:T(8,128)(2,1)S(1)}, bf16[512,1,128]{0,2,1:T(8,128)(2,1)S(1)}, u32[]{:S(2)}, u32[]{:S(2)}) collective-permute-start(bf16[512,1,128]{0,2,1:T(8,128)(2,1)S(1)} %collective-permute-done.11), channel_id=1, source_target_pairs={{0,16},{16,32},{32,48},{48,64},{64,80},{80,96},{96,112},{112,128},... | collective-permute-start | bytes 393224 | tf_op jit(solution)/shard_map/ppermute | solution.py:21
  263.0 46.4 %collective-permute-start.4 = (bf16[512,1,128]{2,0,1:T(8,128)(2,1)S(1)}, bf16[512,1,128]{2,0,1:T(8,128)(2,1)}, u32[]{:S(2)}, u32[]{:S(2)}) collective-permute-start(bf16[512,1,128]{2,0,1:T(8,128)(2,1)S(1)} %collective-permute-done.3), channel_id=1, source_target_pairs={{0,16},{16,32},{32,48},{48,64},{64,80},{80,96},{96,112},{112,128},... | collective-permute-start | bytes 393224 | tf_op jit(solution)/shard_map/ppermute | solution.py:21
  267.3 44.4 %collective-permute-start.13 = (bf16[512,1,128]{0,2,1:T(8,128)(2,1)S(1)}, bf16[512,1,128]{0,2,1:T(8,128)(2,1)}, u32[]{:S(2)}, u32[]{:S(2)}) collective-permute-start(bf16[512,1,128]{0,2,1:T(8,128)(2,1)S(1)} %collective-permute-done.12), channel_id=1, source_target_pairs={{0,16},{16,32},{32,48},{48,64},{64,80},{80,96},{96,112},{112,128},... | collective-permute-start | bytes 393224 | tf_op jit(solution)/shard_map/ppermute | solution.py:21
  309.4 9.7 %collective-permute-start.5 = (bf16[512,1,128]{2,0,1:T(8,128)(2,1)}, bf16[512,1,128]{2,0,1:T(8,128)(2,1)}, u32[]{:S(2)}, u32[]{:S(2)}) collective-permute-start(bf16[512,1,128]{2,0,1:T(8,128)(2,1)} %collective-permute-done.4), channel_id=1, source_target_pairs={{0,16},{16,32},{32,48},{48,64},{64,80},{80,96},{96,112},{112,128},... | collective-permute-start | bytes 393224 | tf_op jit(solution)/shard_map/ppermute | solution.py:21
  311.8 10.5 %collective-permute-start.14 = (bf16[512,1,128]{0,2,1:T(8,128)(2,1)}, bf16[512,1,128]{0,2,1:T(8,128)(2,1)}, u32[]{:S(2)}, u32[]{:S(2)}) collective-permute-start(bf16[512,1,128]{0,2,1:T(8,128)(2,1)} %collective-permute-done.13), channel_id=1, source_target_pairs={{0,16},{16,32},{32,48},{48,64},{64,80},{80,96},{96,112},{112,128},... | collective-permute-start | bytes 393224 | tf_op jit(solution)/shard_map/ppermute | solution.py:21
  319.1 10.4 %collective-permute-start.6 = (bf16[512,1,128]{2,0,1:T(8,128)(2,1)}, bf16[512,1,128]{2,0,1:T(8,128)(2,1)S(1)}, u32[]{:S(2)}, u32[]{:S(2)}) collective-permute-start(bf16[512,1,128]{2,0,1:T(8,128)(2,1)} %collective-permute-done.5), channel_id=1, source_target_pairs={{0,16},{16,32},{32,48},{48,64},{64,80},{80,96},{96,112},{112,128},... | collective-permute-start | bytes 393224 | tf_op jit(solution)/shard_map/ppermute | solution.py:21
  322.2 10.9 %collective-permute-start.15 = (bf16[512,1,128]{0,2,1:T(8,128)(2,1)}, bf16[512,1,128]{0,2,1:T(8,128)(2,1)S(1)}, u32[]{:S(2)}, u32[]{:S(2)}) collective-permute-start(bf16[512,1,128]{0,2,1:T(8,128)(2,1)} %collective-permute-done.14), channel_id=1, source_target_pairs={{0,16},{16,32},{32,48},{48,64},{64,80},{80,96},{96,112},{112,128},... | collective-permute-start | bytes 393224 | tf_op jit(solution)/shard_map/ppermute | solution.py:21
  329.4 9.9 %collective-permute-start.7 = (bf16[512,1,128]{2,0,1:T(8,128)(2,1)S(1)}, bf16[512,1,128]{2,0,1:T(8,128)(2,1)S(1)}, u32[]{:S(2)}, u32[]{:S(2)}) collective-permute-start(bf16[512,1,128]{2,0,1:T(8,128)(2,1)S(1)} %collective-permute-done.6), channel_id=1, source_target_pairs={{0,16},{16,32},{32,48},{48,64},{64,80},{80,96},{96,112},{112,128},... | collective-permute-start | bytes 393224 | tf_op jit(solution)/shard_map/ppermute | solution.py:21
  397.2 100.9 %copy-start = (bf16[512,288]{0,1:T(8,128)(2,1)S(1)}, bf16[512,288]{0,1:T(8,128)(2,1)}, u32[]{:S(2)}) copy-start(bf16[512,288]{0,1:T(8,128)(2,1)} %param.9) | copy-start | bytes 884740
  (22 other events, 474.8 us)
Sparse Core Ops, SparseCore 0:
  9.8 43.6 all-gather.5
  56.1 79.0 all-gather.9
  137.8 76.4 all-gather.7
  216.7 87.6 all-gather.11
  306.9 85.0 all-gather.13
  397.3 70.4 reduce-scatter.1
where the time goes:
time: 508 us; the launch traced here: 507 us
  waiting for transfers between devices  262 us (52%)
  blocking collectives  102 us (20%)
  starting transfers between devices  60 us (12%)
  matrix products  32.7 us (6%)
  other arithmetic  23.6 us (5%)
  between operations  15.6 us (3%)
  local copies, waits for them, and re-layouts  11.4 us (2%)
    all_gather x1, waiting for transfers between devices, shards(): lax.all_gather(w_value, 'seq', axis=0, tiled=True)  71.6 us
    reduce_scatter x1, waiting for transfers between devices, shards(): lax.psum_scatter(group_terms.astype(jnp.bfloat16), 'mp', scatter_dimensio...  67.7 us
    ppermute x16, starting transfers between devices, from_behind(): return lax.ppermute(block, axis, route)  59.8 us
    unnamed x1, blocking collectives  53.1 us
    all_gather x1, waiting for transfers between devices, shards(): lax.all_gather(w_key, 'seq', axis=0, tiled=True)  39.3 us
    all_gather x1, waiting for transfers between devices, shards(): lax.all_gather(w_out, 'seq', axis=1, tiled=True)  37.5 us
    all_gather x1, waiting for transfers between devices, shards(): lax.all_gather(w_query, 'seq', axis=0, tiled=True)  32.8 us
    psum x1, blocking collectives, shards(): square_total = lax.psum(squares, 'mp')  29.2 us
  transfers between devices with their start and end apart: 22, of which 11 were waited for; matrix products, arithmetic and copies ran while one was open for 12% of the time, Pallas kernels for 0%

commit v1 on v0

--- a/solution.py
+++ b/solution.py
@@ -51,7 +51,12 @@
     normed = (x_whole * pre_scale * (1.0 + gain_full.astype(jnp.float32))[None, :]).astype(
         jnp.bfloat16
     )
-    query_raw = add_product(normed, lax.all_gather(w_query, "seq", axis=0, tiled=True))
+    query_raw = add_product(
+        normed,
+        jnp.concatenate(
+            lax.all_to_all(jnp.stack([w_query] * lax.axis_size("seq")), "seq", 0, 0), axis=0
+        ),
+    )
     key_raw = add_product(normed, lax.all_gather(w_key, "seq", axis=0, tiled=True))
     value_raw = add_product(normed, lax.all_gather(w_value, "seq", axis=0, tiled=True))
     heads_query = w_query.shape[1] // HD

time: 508 us -> 459 us (0.904)
  waiting for transfers between devices: 262 us -> 153 us
  blocking collectives: 102 us -> 143 us
  starting transfers between devices: 60 us -> 78.7 us
    pmin x1, blocking collectives: 19.3 us -> 60.7 us  [shards(): starts = lax.pmin(local_first, 'seq')]
    all_gather x1, waiting for transfers between devices: 39.3 us -> 0.01 us  [shards(): lax.all_gather(w_key, 'seq', axis=0, tiled=True)]
    all_gather x1, waiting for transfers between devices: 37.5 us -> 2.49 us  [shards(): lax.all_gather(w_out, 'seq', axis=1, tiled=True)]
    all_gather x1 -> x0, waiting for transfers between devices: 32.8 us -> none  [shards(): lax.all_gather(w_query, 'seq', axis=0, tiled=True)]
    all_to_all x0 -> x1, starting transfers between devices: none -> 11.2 us  [shards(): lax.all_to_all(jnp.stack([w_query] * lax.axis_size('seq')), 'seq', 0, 0)]
    ppermute x16, starting transfers between devices: 59.8 us -> 67.3 us  [from_behind(): return lax.ppermute(block, axis, route)]
  transfers between devices with their start and end apart: 22 -> 22, of which waited for: 11 -> 10; matrix products, arithmetic and copies ran while one was open for 12% -> 13% of each run, Pallas kernels for 0% -> 0%
where the time goes in v1:
time: 459 us; the launch traced here: 458 us
  waiting for transfers between devices  153 us (33%)
  blocking collectives  143 us (31%)
  starting transfers between devices  78.7 us (17%)
  matrix products  32.4 us (7%)
  other arithmetic  22.9 us (5%)
  between operations  15 us (3%)
  local copies, waits for them, and re-layouts  13.1 us (3%)
    reduce_scatter x1, waiting for transfers between devices, shards(): lax.psum_scatter(group_terms.astype(jnp.bfloat16), 'mp', scatter_dimensio...  70.5 us
    all_gather x1, waiting for transfers between devices, shards(): lax.all_gather(w_value, 'seq', axis=0, tiled=True)  67.4 us
    ppermute x16, starting transfers between devices, from_behind(): return lax.ppermute(block, axis, route)  67.3 us
    pmin x1, blocking collectives, shards(): starts = lax.pmin(local_first, 'seq')  60.7 us
    unnamed x1, blocking collectives  53 us
    psum x1, blocking collectives, shards(): square_total = lax.psum(squares, 'mp')  29.2 us
    dot_general x3, matrix products, add_product(): return jnp.dot(normed, piece, preferred_element_type=jnp.float32)  14.2 us
    all_to_all x1, starting transfers between devices, shards(): lax.all_to_all(jnp.stack([w_query] * lax.axis_size('seq')), 'seq', 0, 0)  11.2 us
  transfers between devices with their start and end apart: 22, of which 10 were waited for; matrix products, arithmetic and copies ran while one was open for 13% of the time, Pallas kernels for 0%

profile of v1, /device:TPU:32, one launch (start us, length us, event | category | flops | bytes accessed | tf_op | source)
XLA Modules:
  0.0 458.0 jit_solution(6200327272760096540)
XLA Ops:
  16.1 11.2 %all-to-all-start = ((bf16[16,288,256]{2,1,0:T(8,128)(2,1)}), bf16[16,288,256]{2,1,0:T(8,128)(2,1)S(1)}, u32[]{:S(2)}, u32[]{:S(2)}) async-start(bf16[16,288,256]{2,1,0:T(8,128)(2,1)} %stack.19), calls=%async_computation | async-start | bytes 4718592 | tf_op jit(solution)/shard_map/all_to_all | solution.py:57
  27.3 60.7 %pmin.7 = s32[4]{0:T(128)S(1)} all-reduce(s32[4]{0:T(128)S(1)} %pad_add_fusion), channel_id=1, replica_groups=mesh['seq'=16,'mp'=16] {'seq'}, use_global_device_ids=true, to_apply=%region_5.6 | all-reduce | flops 4 | bytes 32 | tf_op jit(solution)/shard_map/pmin | solution.py:70
  89.5 53.0 %all-reduce = bf16[4608]{0:T(1024)(128)(2,1)S(1)} all-reduce(bf16[4608]{0:T(1024)(128)(2,1)S(1)} %dynamic-update-slice), channel_id=1, replica_groups=mesh['seq'=16,'mp'=16] {'mp'}, use_global_device_ids=true, to_apply=%add | all-reduce | flops 4608 | bytes 18432
  149.0 4.4 convolution_bitcast_fusion
  154.1 5.7 %collective-permute-start.8 = (bf16[512,1,128]{0,2,1:T(8,128)(2,1)S(1)}, bf16[512,1,128]{0,2,1:T(8,128)(2,1)S(1)}, u32[]{:S(2)}, u32[]{:S(2)}) collective-permute-start(bf16[512,1,128]{0,2,1:T(8,128)(2,1)S(1)} %pad_maximum_fusion), channel_id=1, source_target_pairs={{0,16},{16,32},{32,48},{48,64},{64,80},{80,96},{96,112},{112,128},... | collective-permute-start | bytes 393224 | tf_op jit(solution)/shard_map/ppermute | solution.py:21
  159.7 67.4 %all-gather.7.cloned.1.call-done = bf16[4608,128]{1,0:T(8,128)(2,1)} async-done(((bf16[288,128]{1,0:T(8,128)(2,1)}), bf16[4608,128]{1,0:T(8,128)(2,1)}) %all-gather.7.cloned.1.call-update) | async-done | bytes 1179664 | tf_op jit(solution)/shard_map/all_gather | solution.py:61
  227.1 4.8 %convolution_convert_fusion.2 = bf16[512,128]{1,0:T(8,128)(2,1)S(1)} fusion(bf16[4608,128]{1,0:T(8,128)(2,1)} %all-gather.7.cloned.1.call-done, bf16[512,4608]{0,1:T(8,128)(2,1)} %all-gather.5.cloned.1.call-done, f32[4608]{0:T(1024)S(1)} %convert_add_fusion.1, f32[512]{0:T(512)S(1)} %add_rsqrt_fusion.1), kind=kOutput, calls=%fused_computation.26 | convolution fusion | flops 613482496 | bytes 6049792 | tf_op jit(solution)/shard_map/dot_general | solution.py:40
  234.5 5.4 %collective-permute-start.9 = (bf16[512,1,128]{0,2,1:T(8,128)(2,1)S(1)}, bf16[512,1,128]{0,2,1:T(8,128)(2,1)S(1)}, u32[]{:S(2)}, u32[]{:S(2)}) collective-permute-start(bf16[512,1,128]{0,2,1:T(8,128)(2,1)S(1)} %collective-permute-done.8), channel_id=1, source_target_pairs={{0,16},{16,32},{32,48},{48,64},{64,80},{80,96},{96,112},{112,128},... | collective-permute-start | bytes 393224 | tf_op jit(solution)/shard_map/ppermute | solution.py:21
  244.2 5.0 %collective-permute-start.10 = (bf16[512,1,128]{0,2,1:T(8,128)(2,1)S(1)}, bf16[512,1,128]{0,2,1:T(8,128)(2,1)S(1)}, u32[]{:S(2)}, u32[]{:S(2)}) collective-permute-start(bf16[512,1,128]{0,2,1:T(8,128)(2,1)S(1)} %collective-permute-done.9), channel_id=1, source_target_pairs={{0,16},{16,32},{32,48},{48,64},{64,80},{80,96},{96,112},{112,128},... | collective-permute-start | bytes 393224 | tf_op jit(solution)/shard_map/ppermute | solution.py:21
  254.8 3.6 collective-permute-start.11
  260.3 4.3 collective-permute-start.3
  269.1 7.1 %fusion.10 = pred[512,4608]{0,1:T(8,128)(4,1)} fusion(s32[512]{0:T(512)S(1)} %copy-done.7, s32[4608]{0:T(1024)S(1)} %get-tuple-element.62, s32[512]{0:T(512)S(1)} %iota_add_fusion.1, s32[4608]{0:T(1024)S(1)} %get-tuple-element.61, pred[4608]{0:T(1024)(128)(4,1)S(1)} %fusion.54), kind=kLoop, calls=%fused_computation.14 | loop fusion | flops 16515072 | bytes 2404864 | tf_op jit(solution)/shard_map/while/body/eval_jaxpr/and | solution.py:101
  276.2 4.1 collective-permute-start.4
  280.3 5.7 %collective-permute-start.13 = (bf16[512,1,128]{0,2,1:T(8,128)(2,1)}, bf16[512,1,128]{0,2,1:T(8,128)(2,1)}, u32[]{:S(2)}, u32[]{:S(2)}) collective-permute-start(bf16[512,1,128]{0,2,1:T(8,128)(2,1)} %collective-permute-done.12), channel_id=1, source_target_pairs={{0,16},{16,32},{32,48},{48,64},{64,80},{80,96},{96,112},{112,128},... | collective-permute-start | bytes 393224 | tf_op jit(solution)/shard_map/ppermute | solution.py:21
  289.2 3.5 collective-permute-start.5
  292.6 5.1 %collective-permute-start.14 = (bf16[512,1,128]{0,2,1:T(8,128)(2,1)}, bf16[512,1,128]{0,2,1:T(8,128)(2,1)S(1)}, u32[]{:S(2)}, u32[]{:S(2)}) collective-permute-start(bf16[512,1,128]{0,2,1:T(8,128)(2,1)} %collective-permute-done.13), channel_id=1, source_target_pairs={{0,16},{16,32},{32,48},{48,64},{64,80},{80,96},{96,112},{112,128},... | collective-permute-start | bytes 393224 | tf_op jit(solution)/shard_map/ppermute | solution.py:21
  297.8 4.9 %fusion.12 = f32[512,2,128]{0,2,1:T(8,128)S(1)} fusion(bf16[2,128,4608]{2,1,0:T(8,128)(2,1)} %bitcast.98, bf16[512,4608]{0,1:T(8,128)(2,1)} %all-gather.5.cloned.1.call-done, f32[4608]{0:T(1024)} %copy-done.6, f32[512]{0:T(512)S(1)} %add_rsqrt_fusion.1), kind=kOutput, calls=%fused_computation.17 | convolution fusion | flops 1217396736 | bytes 7622656 | tf_op jit(solution)/shard_map/dot_general | solution.py:40
  302.7 4.9 %collective-permute-start.6 = (bf16[512,1,128]{2,0,1:T(8,128)(2,1)S(1)}, bf16[512,1,128]{2,0,1:T(8,128)(2,1)S(1)}, u32[]{:S(2)}, u32[]{:S(2)}) collective-permute-start(bf16[512,1,128]{2,0,1:T(8,128)(2,1)S(1)} %collective-permute-done.5), channel_id=1, source_target_pairs={{0,16},{16,32},{32,48},{48,64},{64,80},{80,96},{96,112},{112,128},... | collective-permute-start | bytes 393224 | tf_op jit(solution)/shard_map/ppermute | solution.py:21
  313.8 6.1 %collective-permute-start.7 = (bf16[512,1,128]{2,0,1:T(8,128)(2,1)S(1)}, bf16[512,1,128]{2,0,1:T(8,128)(2,1)S(1)}, u32[]{:S(2)}, u32[]{:S(2)}) collective-permute-start(bf16[512,1,128]{2,0,1:T(8,128)(2,1)S(1)} %collective-permute-done.6), channel_id=1, source_target_pairs={{0,16},{16,32},{32,48},{48,64},{64,80},{80,96},{96,112},{112,128},... | collective-permute-start | bytes 393224 | tf_op jit(solution)/shard_map/ppermute | solution.py:21
  325.5 6.4 %fusion = (f32[2,512]{1,0:T(2,128)S(1)}, f32[4608,512,2]{1,0,2:T(8,128)S(1)}) fusion(pred[512,4608]{0,1:T(8,128)(4,1)S(1)} %copy-done, f32[512,2,64]{0,2,1:T(8,128)S(1)} %get-tuple-element.42, f32[512,2,64]{0,2,1:T(8,128)S(1)} %get-tuple-element.41, bf16[4608,1,128]{0,2,1:T(8,128)(2,1)S(1)} %constant_dynamic-update-slice_fusion.9), kind=kOutput, calls=%fused_computation.3 | convolution fusion | flops 1227226112 | bytes 22941696 | tf_op jit(solution)/shard_map/while/body/eval_jaxpr/qgrd,kgd->grqk/dot_general | solution.py:106
  331.9 6.3 %fusion.26 = bf16[512,1,2,128]{0,3,2,1:T(8,128)(2,1)S(1)} fusion(f32[4608,512,2]{1,0,2:T(8,128)S(1)} %get-tuple-element.60, pred[512,4608]{0,1:T(8,128)(4,1)S(1)} %copy-done, bf16[4608,1,128]{2,0,1:T(8,128)(2,1)S(1)} %constant_dynamic-update-slice_fusion, f32[512,2]{0,1:T(2,128)S(1)} %bitcast.102), kind=kOutput, calls=%fused_computation.28 | convolution fusion | flops 1227096064 | bytes 22679552 | tf_op jit(solution)/shard_map/while/body/eval_jaxpr/grqk,kgd->qgrd/dot_general | solution.py:111
  340.7 5.2 %convolution_convert_fusion = bf16[512,4608]{0,1:T(8,128)(2,1)} fusion(bf16[256,4608]{0,1:T(8,128)(2,1)} %all-gather.11.cloned.1.call-done, bf16[512,256]{0,1:T(8,128)(2,1)S(1)} %bitcast.101), kind=kOutput, calls=%fused_computation.16 | convolution fusion | flops 1210318848 | bytes 7340032 | tf_op jit(solution)/shard_map/dot_general | solution.py:119
  348.9 70.5 %reduce-scatter.2.cloned.1.call-done = bf16[512,288]{0,1:T(8,128)(2,1)} async-done(((bf16[512,4608]{0,1:T(8,128)(2,1)}), bf16[512,288]{0,1:T(8,128)(2,1)}) %reduce-scatter.2.cloned.1.call-update) | async-done | bytes 294928 | tf_op jit(solution)/shard_map/reduce_scatter | solution.py:124
  420.4 29.2 %psum.7 = f32[512]{0:T(512)S(1)} all-reduce(f32[512]{0:T(512)S(1)} %fusion.31), channel_id=1, replica_groups=mesh['seq'=16,'mp'=16] {'mp'}, use_global_device_ids=true, to_apply=%region_9.10 | all-reduce | flops 512 | bytes 4096 | tf_op jit(solution)/shard_map/psum | solution.py:128
  (111 shorter events, 58.6 us)
Async XLA Ops:
  7.2 138.4 %all-gather.5.cloned.1.call-start = ((), (), s32[]{:S(2)}) async-start(), calls=%async_computation.2 | async-start | bytes 5013504 | tf_op jit(solution)/shard_map/all_gather | solution.py:46
  7.9 141.1 %all-gather.9.cloned.1.call-start = ((), (), s32[]{:S(2)}) async-start(), calls=%async_computation.4 | async-start | bytes 1253376 | tf_op jit(solution)/shard_map/all_gather | solution.py:60
  8.6 218.5 %all-gather.7.cloned.1.call-start = ((), (), s32[]{:S(2)}) async-start(), calls=%async_computation.3 | async-start | bytes 1253376 | tf_op jit(solution)/shard_map/all_gather | solution.py:61
  16.1 270.6 %all-to-all-start = ((bf16[16,288,256]{2,1,0:T(8,128)(2,1)}), bf16[16,288,256]{2,1,0:T(8,128)(2,1)S(1)}, u32[]{:S(2)}, u32[]{:S(2)}) async-start(bf16[16,288,256]{2,1,0:T(8,128)(2,1)} %stack.19), calls=%async_computation | async-start | bytes 4718592 | tf_op jit(solution)/shard_map/all_to_all | solution.py:57
  27.3 313.5 %all-gather.11.cloned.1.call-start = ((), (), s32[]{:S(2)}) async-start(), calls=%async_computation.5 | async-start | bytes 2506752 | tf_op jit(solution)/shard_map/all_gather | solution.py:121
  154.0 115.1 %copy-start.7 = (s32[512]{0:T(512)S(1)}, s32[512]{0:T(512)}, u32[]{:S(2)}) copy-start(s32[512]{0:T(512)} %param.16) | copy-start | bytes 6148
  154.1 80.4 %collective-permute-start.8 = (bf16[512,1,128]{0,2,1:T(8,128)(2,1)S(1)}, bf16[512,1,128]{0,2,1:T(8,128)(2,1)S(1)}, u32[]{:S(2)}, u32[]{:S(2)}) collective-permute-start(bf16[512,1,128]{0,2,1:T(8,128)(2,1)S(1)} %pad_maximum_fusion), channel_id=1, source_target_pairs={{0,16},{16,32},{32,48},{48,64},{64,80},{80,96},{96,112},{112,128},... | collective-permute-start | bytes 393224 | tf_op jit(solution)/shard_map/ppermute | solution.py:21
  232.0 9.3 %collective-permute-start = (bf16[512,1,128]{2,0,1:T(8,128)(2,1)S(1)}, bf16[512,1,128]{2,0,1:T(8,128)(2,1)S(1)}, u32[]{:S(2)}, u32[]{:S(2)}) collective-permute-start(bf16[512,1,128]{2,0,1:T(8,128)(2,1)S(1)} %bitcast.99), channel_id=1, source_target_pairs={{0,16},{16,32},{32,48},{48,64},{64,80},{80,96},{96,112},{112,128},... | collective-permute-start | bytes 393224 | tf_op jit(solution)/shard_map/ppermute | solution.py:21
  234.5 9.7 %collective-permute-start.9 = (bf16[512,1,128]{0,2,1:T(8,128)(2,1)S(1)}, bf16[512,1,128]{0,2,1:T(8,128)(2,1)S(1)}, u32[]{:S(2)}, u32[]{:S(2)}) collective-permute-start(bf16[512,1,128]{0,2,1:T(8,128)(2,1)S(1)} %collective-permute-done.8), channel_id=1, source_target_pairs={{0,16},{16,32},{32,48},{48,64},{64,80},{80,96},{96,112},{112,128},... | collective-permute-start | bytes 393224 | tf_op jit(solution)/shard_map/ppermute | solution.py:21
  241.2 9.3 %collective-permute-start.1 = (bf16[512,1,128]{2,0,1:T(8,128)(2,1)S(1)}, bf16[512,1,128]{2,0,1:T(8,128)(2,1)S(1)}, u32[]{:S(2)}, u32[]{:S(2)}) collective-permute-start(bf16[512,1,128]{2,0,1:T(8,128)(2,1)S(1)} %collective-permute-done), channel_id=1, source_target_pairs={{0,16},{16,32},{32,48},{48,64},{64,80},{80,96},{96,112},{112,128},... | collective-permute-start | bytes 393224 | tf_op jit(solution)/shard_map/ppermute | solution.py:21
  244.2 10.7 %collective-permute-start.10 = (bf16[512,1,128]{0,2,1:T(8,128)(2,1)S(1)}, bf16[512,1,128]{0,2,1:T(8,128)(2,1)S(1)}, u32[]{:S(2)}, u32[]{:S(2)}) collective-permute-start(bf16[512,1,128]{0,2,1:T(8,128)(2,1)S(1)} %collective-permute-done.9), channel_id=1, source_target_pairs={{0,16},{16,32},{32,48},{48,64},{64,80},{80,96},{96,112},{112,128},... | collective-permute-start | bytes 393224 | tf_op jit(solution)/shard_map/ppermute | solution.py:21
  249.2 170.2 %reduce-scatter.2.cloned.1.call-start = ((), (), s32[]{:S(2)}) async-start(), calls=%async_computation.6 | async-start | bytes 5013504 | tf_op jit(solution)/shard_map/reduce_scatter | solution.py:124
  250.5 9.8 %collective-permute-start.2 = (bf16[512,1,128]{2,0,1:T(8,128)(2,1)S(1)}, bf16[512,1,128]{2,0,1:T(8,128)(2,1)S(1)}, u32[]{:S(2)}, u32[]{:S(2)}) collective-permute-start(bf16[512,1,128]{2,0,1:T(8,128)(2,1)S(1)} %collective-permute-done.1), channel_id=1, source_target_pairs={{0,16},{16,32},{32,48},{48,64},{64,80},{80,96},{96,112},{112,128},... | collective-permute-start | bytes 393224 | tf_op jit(solution)/shard_map/ppermute | solution.py:21
  254.8 10.9 %collective-permute-start.11 = (bf16[512,1,128]{0,2,1:T(8,128)(2,1)S(1)}, bf16[512,1,128]{0,2,1:T(8,128)(2,1)S(1)}, u32[]{:S(2)}, u32[]{:S(2)}) collective-permute-start(bf16[512,1,128]{0,2,1:T(8,128)(2,1)S(1)} %collective-permute-done.10), channel_id=1, source_target_pairs={{0,16},{16,32},{32,48},{48,64},{64,80},{80,96},{96,112},{112,128},... | collective-permute-start | bytes 393224 | tf_op jit(solution)/shard_map/ppermute | solution.py:21
  260.3 15.9 %collective-permute-start.3 = (bf16[512,1,128]{2,0,1:T(8,128)(2,1)S(1)}, bf16[512,1,128]{2,0,1:T(8,128)(2,1)}, u32[]{:S(2)}, u32[]{:S(2)}) collective-permute-start(bf16[512,1,128]{2,0,1:T(8,128)(2,1)S(1)} %collective-permute-done.2), channel_id=1, source_target_pairs={{0,16},{16,32},{32,48},{48,64},{64,80},{80,96},{96,112},{112,128},... | collective-permute-start | bytes 393224 | tf_op jit(solution)/shard_map/ppermute | solution.py:21
  265.7 14.6 %collective-permute-start.12 = (bf16[512,1,128]{0,2,1:T(8,128)(2,1)S(1)}, bf16[512,1,128]{0,2,1:T(8,128)(2,1)}, u32[]{:S(2)}, u32[]{:S(2)}) collective-permute-start(bf16[512,1,128]{0,2,1:T(8,128)(2,1)S(1)} %collective-permute-done.11), channel_id=1, source_target_pairs={{0,16},{16,32},{32,48},{48,64},{64,80},{80,96},{96,112},{112,128},... | collective-permute-start | bytes 393224 | tf_op jit(solution)/shard_map/ppermute | solution.py:21
  276.2 13.0 %collective-permute-start.4 = (bf16[512,1,128]{2,0,1:T(8,128)(2,1)}, bf16[512,1,128]{2,0,1:T(8,128)(2,1)}, u32[]{:S(2)}, u32[]{:S(2)}) collective-permute-start(bf16[512,1,128]{2,0,1:T(8,128)(2,1)} %collective-permute-done.3), channel_id=1, source_target_pairs={{0,16},{16,32},{32,48},{48,64},{64,80},{80,96},{96,112},{112,128},... | collective-permute-start | bytes 393224 | tf_op jit(solution)/shard_map/ppermute | solution.py:21
  280.3 12.3 %collective-permute-start.13 = (bf16[512,1,128]{0,2,1:T(8,128)(2,1)}, bf16[512,1,128]{0,2,1:T(8,128)(2,1)}, u32[]{:S(2)}, u32[]{:S(2)}) collective-permute-start(bf16[512,1,128]{0,2,1:T(8,128)(2,1)} %collective-permute-done.12), channel_id=1, source_target_pairs={{0,16},{16,32},{32,48},{48,64},{64,80},{80,96},{96,112},{112,128},... | collective-permute-start | bytes 393224 | tf_op jit(solution)/shard_map/ppermute | solution.py:21
  289.2 13.6 %collective-permute-start.5 = (bf16[512,1,128]{2,0,1:T(8,128)(2,1)}, bf16[512,1,128]{2,0,1:T(8,128)(2,1)S(1)}, u32[]{:S(2)}, u32[]{:S(2)}) collective-permute-start(bf16[512,1,128]{2,0,1:T(8,128)(2,1)} %collective-permute-done.4), channel_id=1, source_target_pairs={{0,16},{16,32},{32,48},{48,64},{64,80},{80,96},{96,112},{112,128},... | collective-permute-start | bytes 393224 | tf_op jit(solution)/shard_map/ppermute | solution.py:21
  292.6 15.0 %collective-permute-start.14 = (bf16[512,1,128]{0,2,1:T(8,128)(2,1)}, bf16[512,1,128]{0,2,1:T(8,128)(2,1)S(1)}, u32[]{:S(2)}, u32[]{:S(2)}) collective-permute-start(bf16[512,1,128]{0,2,1:T(8,128)(2,1)} %collective-permute-done.13), channel_id=1, source_target_pairs={{0,16},{16,32},{32,48},{48,64},{64,80},{80,96},{96,112},{112,128},... | collective-permute-start | bytes 393224 | tf_op jit(solution)/shard_map/ppermute | solution.py:21
  302.7 11.0 %collective-permute-start.6 = (bf16[512,1,128]{2,0,1:T(8,128)(2,1)S(1)}, bf16[512,1,128]{2,0,1:T(8,128)(2,1)S(1)}, u32[]{:S(2)}, u32[]{:S(2)}) collective-permute-start(bf16[512,1,128]{2,0,1:T(8,128)(2,1)S(1)} %collective-permute-done.5), channel_id=1, source_target_pairs={{0,16},{16,32},{32,48},{48,64},{64,80},{80,96},{96,112},{112,128},... | collective-permute-start | bytes 393224 | tf_op jit(solution)/shard_map/ppermute | solution.py:21
  307.6 12.2 %collective-permute-start.15 = (bf16[512,1,128]{0,2,1:T(8,128)(2,1)S(1)}, bf16[512,1,128]{0,2,1:T(8,128)(2,1)S(1)}, u32[]{:S(2)}, u32[]{:S(2)}) collective-permute-start(bf16[512,1,128]{0,2,1:T(8,128)(2,1)S(1)} %collective-permute-done.14), channel_id=1, source_target_pairs={{0,16},{16,32},{32,48},{48,64},{64,80},{80,96},{96,112},{112,128},... | collective-permute-start | bytes 393224 | tf_op jit(solution)/shard_map/ppermute | solution.py:21
  313.8 9.7 %collective-permute-start.7 = (bf16[512,1,128]{2,0,1:T(8,128)(2,1)S(1)}, bf16[512,1,128]{2,0,1:T(8,128)(2,1)S(1)}, u32[]{:S(2)}, u32[]{:S(2)}) collective-permute-start(bf16[512,1,128]{2,0,1:T(8,128)(2,1)S(1)} %collective-permute-done.6), channel_id=1, source_target_pairs={{0,16},{16,32},{32,48},{48,64},{64,80},{80,96},{96,112},{112,128},... | collective-permute-start | bytes 393224 | tf_op jit(solution)/shard_map/ppermute | solution.py:21
  345.9 103.7 %copy-start.1 = (bf16[512,288]{0,1:T(8,128)(2,1)S(1)}, bf16[512,288]{0,1:T(8,128)(2,1)}, u32[]{:S(2)}) copy-start(bf16[512,288]{0,1:T(8,128)(2,1)} %param.9) | copy-start | bytes 884740
  (10 other events, 320.8 us)
Sparse Core Ops, SparseCore 0:
  9.8 47.5 all-gather.4
  60.1 87.9 all-gather.8
  150.7 76.4 all-gather.6
  249.3 91.3 all-gather.10
  346.1 73.2 reduce-scatter.1
